TPU v7x, 256 devices: a whole 4x4x8 slice. The times are simulated.
256 devices in a mesh: dp: 8 (over z_hi, x), row: 4 (over y), col: 8 (over z_lo, core).
Axes of the slice: x: 4, y: 4, z: 8 (z_hi: 2, z_lo: 4; z = z_hi * 4 + z_lo), core: 2. Of those that a mesh axis runs over, the one named last changes fastest.
Arguments:
- acts: bfloat16 [4096, 8192], P(('dp', 'col'), 'row'), may hold values from -0.25 to 0.25
- grad_out: bfloat16 [4096, 14336], P(('dp', 'row'), 'col'), may hold values from -6 to 6
- weight: bfloat16 [8192, 14336], P('row', 'col'), may hold values from -0.0625 to 0.0625
Outputs:
- grad_input: bfloat16 [4096, 8192], P(('dp', 'col'), 'row')
- grad_weight: bfloat16 [4, 2048, 14336], P('row', 'dp', 'col')
All inputs are finite; a program needn't handle non-finite values.
Results may differ from a plain program's by a relative error of at most 0.001.
Values may be sent and summed in bfloat16 or wider, within the bound.
A program may use at most 128 MiB of HBM per device.

v0:
```python
import jax
import jax.numpy as jnp
from jax import lax
from jax.sharding import PartitionSpec as P


def shards(acts, grad_out, weight):
    act_local = lax.all_gather(acts, "col", axis=0, tiled=True)
    partial_value = lax.dot_general(
        lax.all_gather(grad_out, "row", axis=0, tiled=True),
        weight,
        (((1,), (1,)), ((), ())),
        preferred_element_type=jnp.float32,
    )
    act_all = lax.all_to_all(act_local, "dp", split_axis=1, concat_axis=0, tiled=True)
    summed = lax.dot_general(
        act_all,
        lax.all_gather(grad_out, ("dp", "row"), axis=0, tiled=True),
        (((0,), (0,)), ((), ())),
        preferred_element_type=jnp.float32,
    )
    grad_weight = summed.astype(jnp.bfloat16)[None]
    grad_input = lax.psum_scatter(partial_value, "col", scatter_dimension=0, tiled=True).astype(
        jnp.bfloat16
    )
    return (grad_input, grad_weight)


def solution(mesh):
    in_specs = (P(("dp", "col"), "row"), P(("dp", "row"), "col"), P("row", "col"))
    out_specs = (P(("dp", "col"), "row"), P("row", "dp", "col"))
    return jax.shard_map(shards, mesh=mesh, in_specs=in_specs, out_specs=out_specs, check_vma=False)
```

profile of v0, /device:TPU:1, one launch (start us, length us, event | category | flops | bytes accessed | tf_op | source)
XLA Modules:
  0.0 420.8 jit_solution(18162088527269085806)
XLA Ops:
  7.2 0.0 all-gather.4.cloned.1.call-start
  7.2 0.7 all-gather.4.cloned.1.call-update
  7.9 0.0 all-gather.6.cloned.1.call-start
  7.9 0.7 all-gather.6.cloned.1.call-update
  8.6 0.0 reduce-scatter.2.cloned.1.call-start
  8.7 36.2 %all-gather.4.cloned.1.call-done = bf16[512,1792]{1,0:T(8,128)(2,1)} async-done(((bf16[128,1792]{1,0:T(8,128)(2,1)}), bf16[512,1792]{1,0:T(8,128)(2,1)}) %all-gather.4.cloned.1.call-update) | async-done | bytes 1835024 | tf_op jit(solution)/shard_map/all_gather | solution.py:10
  44.9 9.6 %fusion.1 = f32[512,2048]{1,0:T(8,128)} fusion(bf16[512,1792]{1,0:T(8,128)(2,1)} %all-gather.4.cloned.1.call-done, bf16[2048,1792]{1,0:T(8,128)(2,1)} %param.5), kind=kOutput, calls=%fused_computation.2 | convolution fusion | flops 3758096384 | bytes 13369344 | tf_op jit(solution)/shard_map/dot_general | solution.py:9
  54.5 0.0 reduce-scatter.2.cloned.1.call-update
  54.5 0.0 all-gather.8.cloned.1.call-start
  54.6 0.5 all-gather.8.cloned.1.call-update
  55.1 29.2 %all-gather.6.cloned.1.call-done = bf16[512,2048]{1,0:T(8,128)(2,1)} async-done(((bf16[64,2048]{1,0:T(8,128)(2,1)}), bf16[512,2048]{1,0:T(8,128)(2,1)}) %all-gather.6.cloned.1.call-update) | async-done | bytes 2097168 | tf_op jit(solution)/shard_map/all_gather | solution.py:8
  84.3 2.9 copy.7
  87.1 70.2 %all_to_all.19 = bf16[512,8,256]{0,2,1:T(8,128)(2,1)} all-to-all(bf16[512,8,256]{0,2,1:T(8,128)(2,1)S(1)} %bitcast.10), channel_id=1, replica_groups=mesh['dp'=8,'row'=4,'col'=8] {'dp'}, dimensions={1} | all-to-all | bytes 4194304 | tf_op jit(solution)/shard_map/all_to_all | solution.py:15
  157.3 2.9 copy.8
  160.2 20.1 %reduce-scatter.2.cloned.1.call-done = f32[64,2048]{1,0:T(8,128)} async-done(((f32[512,2048]{1,0:T(8,128)}), f32[64,2048]{1,0:T(8,128)}) %reduce-scatter.2.cloned.1.call-update) | async-done | bytes 524304 | tf_op jit(solution)/shard_map/reduce_scatter | solution.py:23
  180.3 1.8 convert_element_type.6
  182.0 223.9 %all-gather.8.cloned.1.call-done = bf16[4096,1792]{1,0:T(8,128)(2,1)} async-done(((bf16[128,1792]{1,0:T(8,128)(2,1)}), bf16[4096,1792]{1,0:T(8,128)(2,1)}) %all-gather.8.cloned.1.call-update) | async-done | bytes 14680080 | tf_op jit(solution)/shard_map/all_gather | solution.py:18
  406.0 8.3 %fusion = bf16[1,256,1792]{2,1,0:T(8,128)(2,1)} fusion(bf16[4096,256]{1,0:T(8,128)(2,1)S(1)} %bitcast.9, bf16[4096,1792]{1,0:T(8,128)(2,1)} %all-gather.8.cloned.1.call-done), kind=kOutput, calls=%fused_computation.1 | convolution fusion | flops 3758555136 | bytes 17694720 | tf_op jit(solution)/shard_map/dot_general | solution.py:16
Async XLA Ops:
  7.2 37.7 %all-gather.4.cloned.1.call-start = ((), (), s32[]{:S(2)}) async-start(), calls=%async_computation.2 | async-start | bytes 2293760 | tf_op jit(solution)/shard_map/all_gather | solution.py:10
  7.9 76.4 %all-gather.6.cloned.1.call-start = ((), (), s32[]{:S(2)}) async-start(), calls=%async_computation.4 | async-start | bytes 2359296 | tf_op jit(solution)/shard_map/all_gather | solution.py:8
  8.6 171.6 %reduce-scatter.2.cloned.1.call-start = ((), (), s32[]{:S(2)}) async-start(), calls=%async_computation.3 | async-start | bytes 4718592 | tf_op jit(solution)/shard_map/reduce_scatter | solution.py:23
  54.5 351.5 %all-gather.8.cloned.1.call-start = ((), (), s32[]{:S(2)}) async-start(), calls=%async_computation.5 | async-start | bytes 15138816 | tf_op jit(solution)/shard_map/all_gather | solution.py:18
Sparse Core Ops, SparseCore 0:
  9.8 35.0 all-gather.3
  46.7 37.5 all-gather.5
  86.8 93.3 reduce-scatter.1
  183.5 222.4 all-gather.7
where the time goes:
time: 421 us
  waiting for transfers between devices  311 us (74%)
  blocking collectives  70.2 us (17%)
  matrix products  17.9 us (4%)
  between operations  13.8 us (3%)
  local copies, waits for them, and re-layouts  5.72 us (1%)
    all_gather x1, waiting for transfers between devices, shards(): lax.all_gather(grad_out, ('dp', 'row'), axis=0, tiled=True)  224 us
    all_to_all x1, blocking collectives, shards(): lax.all_to_all(act_local, 'dp', split_axis=1, concat_axis=0, tiled=True)  70.2 us
    all_gather x1, waiting for transfers between devices, shards(): lax.all_gather(grad_out, 'row', axis=0, tiled=True)  36.2 us
    all_gather x1, waiting for transfers between devices, shards(): act_local = lax.all_gather(acts, 'col', axis=0, tiled=True)  29.2 us
    reduce_scatter x1, waiting for transfers between devices, shards(): lax.psum_scatter(partial_value, 'col', scatter_dimension=0, tiled=True)  20.1 us
    dot_general x1, matrix products, shards(): lax.dot_general(lax.all_gather(grad_out, 'row', axis=0, tiled=True), weig...  9.6 us
  transfers between devices with their start and end apart: 4, of which 4 were waited for; matrix products, arithmetic and copies ran while one was open for 4% of the time, Pallas kernels for 0%

commit v1 on v0

v1 whole, which is shorter than its diff:
```python
import functools

import jax
import jax.numpy as jnp
from jax import lax
from jax.experimental import pallas as pl
from jax.experimental.pallas import tpu as pltpu
from jax.sharding import PartitionSpec as P

MESH = pl.DeviceIdType.MESH
F32 = jnp.float32
BF16 = jnp.bfloat16
NX = NY = NL = 4
NH = 2
NZ = NH * NL
TILE = 256


class Ring:
    def __init__(self, slot, loc, me, n, dev, send_sem, recv_sem):
        self.slot, self.loc, self.dev = slot, loc, dev
        self.me = me
        self.left, self.right, self.far = (lax.rem(me + s, n) for s in (n - 1, 1, 2))
        self.sends, self.recvs = send_sem, recv_sem

    def _copy(self, ref, k, to):
        i = self.slot * 4 + k
        return pltpu.make_async_remote_copy(
            ref, ref, self.sends.at[i], self.recvs.at[i], device_id=self.dev(to), device_id_type=MESH
        )

    def _half(self, o, k):
        ref = self.loc(o)
        rows = ref.shape[0] // 2
        return ref.at[pl.ds(k * rows, rows)]

    def own(self):
        self._copy(self.loc(self.me), 0, self.right).start()
        self._copy(self.loc(self.me), 1, self.left).start()

    def from_left(self):
        self._copy(self.loc(self.left), 0, self.right).wait_recv()
        self._copy(self._half(self.left, 0), 2, self.right).start()

    def from_right(self):
        self._copy(self.loc(self.right), 1, self.left).wait_recv()
        self._copy(self._half(self.right, 1), 3, self.left).start()

    def from_far(self):
        self._copy(self._half(self.far, 0), 2, self.right).wait_recv()
        self._copy(self._half(self.far, 1), 3, self.left).wait_recv()

    def wait_sent(self):
        self._copy(self.loc(self.me), 0, self.right).wait_send()
        self._copy(self.loc(self.me), 1, self.left).wait_send()
        self._copy(self._half(self.left, 0), 2, self.right).wait_send()
        self._copy(self._half(self.right, 1), 3, self.left).wait_send()


def kernel(
    acts_hbm, grad_hbm, w_hbm, gi_ref, gw_ref,
    gp, gq, w, acts, xbuf, aall, at, acc, lhs, part, pair, near, mid,
    ring_send, ring_recv, loc_sem, hx_send, hx_recv, ax_send, ax_recv, az_send, az_recv,
    ac_send, ac_recv, pr_send, pr_recv, rs_send, rs_recv,
):
    dp, y, col = lax.axis_index("dp"), lax.axis_index("row"), lax.axis_index("col")
    h, x, l, c = dp // NX, dp % NX, col // 2, col % 2
    z = h * NL + l
    oh = 1 - h
    half = gp.shape[3]
    kb = acts.shape[1] // NZ
    nk = part.shape[4]

    def dev_x(to):
        return (h * NX + to, y, col)

    def dev_y(to):
        return (dp, to, col)

    def at_z(s):
        return lax.rem(z + s, NZ)

    def dev_z(s):
        to = at_z(s)
        return ((to // NL) * NX + x, y, (to % NL) * 2 + c)

    pal = (dp, y, l * 2 + 1 - c)

    own_p = pltpu.make_async_copy(grad_hbm.at[pl.ds(0, half)], gp.at[h, x, y], loc_sem.at[0])
    own_q = pltpu.make_async_copy(grad_hbm.at[pl.ds(half, half)], gq.at[h, y, x], loc_sem.at[1])
    own_a = pltpu.make_async_copy(acts_hbm, acts, loc_sem.at[2])
    own_w = pltpu.make_async_copy(w_hbm, w, loc_sem.at[3])
    own_a.start()
    own_p.start()
    own_q.start()
    own_w.start()

    barrier = pltpu.get_barrier_semaphore()
    peers = [dev_x(lax.rem(x + s, NX)) for s in range(1, NX)]
    peers += [dev_y(lax.rem(y + s, NY)) for s in (1, NY - 1)]
    peers += [dev_z(s) for s in range(1, NZ)] + [pal]
    for peer in peers:
        pl.semaphore_signal(barrier, inc=1, device_id=peer, device_id_type=MESH)
    own_a.wait()
    own_p.wait()
    own_q.wait()
    pl.semaphore_wait(barrier, len(peers))

    sent = []

    hx_p = pltpu.make_async_remote_copy(
        gp.at[h, x, y], gp.at[h, x, y], hx_send.at[0], hx_recv.at[0], device_id=dev_z(NL), device_id_type=MESH
    )
    hx_q = pltpu.make_async_remote_copy(
        gq.at[h, y, x], gq.at[h, y, x], hx_send.at[1], hx_recv.at[1], device_id=dev_z(NL), device_id_type=MESH
    )
    ax = []
    for s in range(1, NX):
        to = lax.rem(x + s, NX)
        for b in range(NH):
            i = (s - 1) * NH + b
            cols = pl.ds(pl.multiple_of((b * NX + to) * kb, kb), kb)
            cp = pltpu.make_async_remote_copy(
                acts.at[:, cols], xbuf.at[b, x], ax_send.at[i], ax_recv.at[i],
                device_id=dev_x(to), device_id_type=MESH,
            )
            cp.start()
            ax.append(cp)
    hx_p.start()
    hx_q.start()
    sent += ax + [hx_p, hx_q]
    for b in range(NH):
        cols = pl.ds(pl.multiple_of((b * NX + x) * kb, kb), kb)
        xbuf[b, x] = acts[:, cols]

    slot = iter(range(20))

    def ring(axis, loc):
        me, dev = (x, dev_x) if axis == "x" else (y, dev_y)
        return Ring(next(slot), loc, me, NX, dev, ring_send, ring_recv)

    def p1(b):
        return ring("x", lambda o: gp.at[b, o, y])

    def p2(b, i):
        return ring("y", lambda o: gp.at[b, i, o])

    def q1(b):
        return ring("y", lambda o: gq.at[b, o, x])

    def q2(b, i):
        return ring("x", lambda o: gq.at[b, i, o])

    xs = [x, lax.rem(x + NX - 1, NX), lax.rem(x + 1, NX), lax.rem(x + 2, NX)]
    ys = [y, lax.rem(y + NY - 1, NY), lax.rem(y + 1, NY), lax.rem(y + 2, NY)]
    pa, qa = [p1(h), p1(oh)], [q1(h), q1(oh)]
    pb = [[p2(b, i) for i in xs] for b in (h, oh)]
    qb = [[q2(b, i) for i in ys] for b in (h, oh)]

    acc[...] = jnp.zeros_like(acc)

    def group(is_p, b, i):
        if is_p:
            a = jnp.concatenate([aall[0, b * NL + j, i] for j in range(NY)], axis=0)
            g = gp.at[b, i]
        else:
            a = aall[1, b * NL + i].reshape(NX * half, kb)
            g = gq.at[b, i]
        at[...] = a.astype(F32).T.astype(BF16)

        @pl.loop(0, acc.shape[1] // TILE)
        def _(t):
            n = pl.ds(pl.multiple_of(t * TILE, TILE), TILE)
            acc[:, n] += jnp.dot(at[...], g[:, :, n].reshape(NX * half, TILE), preferred_element_type=F32)

    def lr(r):
        r.from_left()
        r.from_right()

    def grow(first, second):
        first.from_left()
        second[1].own()
        first.from_right()
        second[2].own()

    pa[0].own()
    qa[0].own()
    pb[0][0].own()
    qb[0][0].own()

    for cp in ax:
        cp.wait_recv()
    az = []
    for s in (1, NZ - 1, 2, NZ - 2, 3, NZ - 3, 4):
        b = at_z(s) // NL
        cp = pltpu.make_async_remote_copy(
            xbuf.at[b], aall.at[c, z], az_send.at[s - 1], az_recv.at[s - 1],
            device_id=dev_z(s), device_id_type=MESH,
        )
        cp.start()
        az.append(cp)
    aall[c, z] = xbuf[h]

    def to_pal(s):
        ref = aall.at[c, at_z(s)]
        return pltpu.make_async_remote_copy(
            ref, ref, ac_send.at[s], ac_recv.at[s], device_id=pal, device_id_type=MESH
        )

    def from_pal(s):
        ref = aall.at[1 - c, at_z(s)]
        return pltpu.make_async_remote_copy(
            ref, ref, ac_send.at[s], ac_recv.at[s], device_id=pal, device_id_type=MESH
        )

    to_pal(0).start()

    grow(pa[0], pb[0])
    grow(qa[0], qb[0])
    lr(pb[0][0])
    lr(qb[0][0])
    pa[0].from_far()
    pb[0][3].own()
    qa[0].from_far()
    qb[0][3].own()
    for i in (1, 2):
        lr(pb[0][i])
        lr(qb[0][i])
    hx_p.wait_recv()
    pa[1].own()
    pb[1][0].own()
    hx_q.wait_recv()
    qa[1].own()
    qb[1][0].own()
    lr(pb[0][3])
    lr(qb[0][3])

    for s in range(1, NZ):
        ref = aall.at[c, at_z(NZ - s)]
        pltpu.make_async_remote_copy(
            ref, ref, az_send.at[s - 1], az_recv.at[s - 1], device_id=dev_z(s), device_id_type=MESH
        ).wait_recv()
        to_pal(NZ - s).start()

    grow(pa[1], pb[1])
    grow(qa[1], qb[1])
    lr(pb[1][0])
    lr(qb[1][0])
    pa[1].from_far()
    pb[1][3].own()
    qa[1].from_far()
    qb[1][3].own()

    pb[0][0].from_far()
    pb[1][0].from_far()
    for d, s in enumerate((2, 0, 1, NZ - 1, NZ - 2)):
        to = at_z(s)
        lhs[0, d] = gp[to // NL, x, to % NL]
        lhs[1, d] = gq[to // NL, to % NL, x]
    own_w.wait()

    def partial(k):
        @pl.loop(0, nk // TILE)
        def _(t):
            cols = pl.ds(pl.multiple_of(t * TILE, TILE), TILE)
            rows = pl.ds(pl.multiple_of(k * nk + t * TILE, TILE), TILE)
            both = lhs[:, k : k + 4].reshape(8 * half, lhs.shape[3])
            r = lax.dot_general(both, w[rows], (((1,), (1,)), ((), ())), preferred_element_type=F32)
            part[:, k, :, :, cols] = r.reshape(2, 4, half, TILE)

    def pair_copy(k):
        return pltpu.make_async_remote_copy(
            part.at[1 - c, k], pair.at[k], pr_send.at[k], pr_recv.at[k], device_id=pal, device_id_type=MESH
        )

    def scatter(k):
        pair_copy(k).wait_recv()
        part[c, k] += pair[k]
        todo = (((0, 2, mid.at[0]), (2, 1, near.at[0, 0]), (3, NZ - 1, near.at[1, 0])) if k == 0 else
                ((3, NZ - 2, mid.at[1]), (1, 1, near.at[0, 1]), (2, NZ - 1, near.at[1, 1])))
        out = []
        for i, (d, s, dst) in enumerate(todo):
            cp = pltpu.make_async_remote_copy(
                part.at[c, k, d], dst, rs_send.at[k * 3 + i], rs_recv.at[k * 3 + i],
                device_id=dev_z(s), device_id_type=MESH,
            )
            cp.start()
            out.append(cp)
        return out

    partial(0)
    pair_copy(0).start()
    lr(pb[1][1])
    lr(qb[1][1])
    rs = scatter(0)
    partial(1)
    pair_copy(1).start()
    lr(pb[1][2])
    lr(qb[1][2])
    rs += scatter(1)

    for s in range(NZ):
        from_pal(s).wait_recv()
    for i in range(1, 4):
        pb[0][i].from_far()
    for i in range(4):
        qb[0][i].from_far()
        group(True, h, xs[i])
        if i == 1:
            lr(pb[1][3])
            lr(qb[1][3])
    for i in range(4):
        group(False, h, ys[i])
    for i in range(4):
        if i:
            pb[1][i].from_far()
        group(True, oh, xs[i])
        qb[1][i].from_far()
        group(False, oh, ys[i])

    for cp in rs:
        cp.wait_recv()
    gi_ref[:, :nk] = (part[c, 0, 1] + mid[0] + near[0, 0] + near[1, 0]).astype(BF16)
    gi_ref[:, nk:] = (part[c, 1, 0] + mid[1] + near[0, 1] + near[1, 1]).astype(BF16)
    gw_ref[0] = acc[...].astype(BF16)

    for r in pa + qa + pb[0] + pb[1] + qb[0] + qb[1]:
        r.wait_sent()
    for cp in sent + az + rs:
        cp.wait_send()
    for s in range(NZ):
        to_pal(s).wait_send()
    pair_copy(0).wait_send()
    pair_copy(1).wait_send()


def shards(acts, grad_out, weight):
    frames, width = acts.shape
    rows, hidden = grad_out.shape
    half = rows // 2
    kb = width // NZ
    nk = width // 2
    dma = pltpu.SemaphoreType.DMA
    return pl.pallas_call(
        kernel,
        out_shape=(
            jax.ShapeDtypeStruct((frames, width), BF16),
            jax.ShapeDtypeStruct((1, kb, hidden), BF16),
        ),
        in_specs=[pl.BlockSpec(memory_space=pl.ANY)] * 3,
        out_specs=(pl.BlockSpec(memory_space=pltpu.VMEM),) * 2,
        scratch_shapes=[
            pltpu.VMEM((NH, NX, NY, half, hidden), BF16),
            pltpu.VMEM((NH, NY, NX, half, hidden), BF16),
            pltpu.VMEM((width, hidden), BF16),
            pltpu.VMEM((frames, width), BF16),
            pltpu.VMEM((NH, NX, frames, kb), BF16),
            pltpu.VMEM((2, NZ, NX, frames, kb), BF16),
            pltpu.VMEM((kb, NX * half), BF16),
            pltpu.VMEM((kb, hidden), F32),
            pltpu.VMEM((2, 5, half, hidden), BF16),
            pltpu.VMEM((2, 2, 4, half, nk), F32),
            pltpu.VMEM((2, 4, half, nk), F32),
            pltpu.VMEM((2, 2, half, nk), F32),
            pltpu.VMEM((2, half, nk), F32),
            dma((80,)), dma((80,)), dma((4,)), dma((2,)), dma((2,)), dma((6,)), dma((6,)),
            dma((7,)), dma((7,)), dma((8,)), dma((8,)), dma((2,)), dma((2,)), dma((6,)), dma((6,)),
        ],
        compiler_params=pltpu.CompilerParams(
            collective_id=0, has_side_effects=True, vmem_limit_bytes=62 << 20
        ),
        name="grads",
    )(acts, grad_out, weight)


def solution(mesh):
    in_specs = (P(("dp", "col"), "row"), P(("dp", "row"), "col"), P("row", "col"))
    out_specs = (P(("dp", "col"), "row"), P("row", "dp", "col"))
    return jax.shard_map(shards, mesh=mesh, in_specs=in_specs, out_specs=out_specs, check_vma=False)
```

time: 421 us -> 117 us (0.28)
  waiting for transfers between devices: 311 us -> 0 us
  Pallas kernels: 0 us -> 112 us
  blocking collectives: 70.2 us -> 0 us
  matrix products: 17.9 us -> 0 us
  between operations: 13.8 us -> 0.64 us
    all_gather x3 -> x0, waiting for transfers between devices: 289 us -> none  [the longest x1 224 us: shards(): lax.all_gather(grad_out, ('dp', 'row'), axis=0, tiled=True)]
    pallas_call x0 -> x1, Pallas kernels: none -> 112 us  [shards(): pl.pallas_call(kernel, out_shape=(jax.ShapeDtypeStruct((frames, width), B...]
    all_to_all x1 -> x0, blocking collectives: 70.2 us -> none  [shards(): lax.all_to_all(act_local, 'dp', split_axis=1, concat_axis=0, tiled=True)]
    reduce_scatter x1 -> x0, waiting for transfers between devices: 20.1 us -> none  [shards(): lax.psum_scatter(partial_value, 'col', scatter_dimension=0, tiled=True)]
    dot_general x2 -> x0, matrix products: 17.9 us -> none  [the longest x1 9.6 us: shards(): lax.dot_general(lax.all_gather(grad_out, 'row', axis=0, tiled=True), weig...]
  transfers between devices with their start and end apart: 4 -> 0, of which waited for: 4 -> 0; matrix products, arithmetic and copies ran while one was open for 4% -> 0% of each run, Pallas kernels for 0% -> 0%
where the time goes in v1:
time: 117 us; the launch traced here: 116 us
  Pallas kernels  112 us (96%)
  local copies, waits for them, and re-layouts  3.83 us (3%)
    pallas_call x1, Pallas kernels, shards(): pl.pallas_call(kernel, out_shape=(jax.ShapeDtypeStruct((frames, width), B...  112 us
    unnamed x2, local copies, waits for them, and re-layouts  3.83 us

profile of v1, /device:TPU:1, one launch (start us, length us, event | category | flops | bytes accessed | tf_op | source)
XLA Modules:
  0.0 116.2 jit_solution(840985472933972656)
XLA Ops:
  0.6 111.7 %grads.1 = (bf16[64,2048]{1,0:T(8,128)(2,1)}, bf16[1,256,1792]{2,1,0:T(8,128)(2,1)}) custom-call(bf16[64,2048]{1,0:T(8,128)(2,1)} %acts_hbm.1, bf16[128,1792]{1,0:T(8,128)(2,1)} %grad_hbm.1, bf16[2048,1792]{1,0:T(8,128)(2,1)} %w_hbm.1), custom_call_target="tpu_custom_call" | custom-call | tf_op jit(solution)/shard_map/grads/pallas_call | solution.py:344
  112.3 1.7 %copy.7 = bf16[64,2048]{1,0:T(8,128)(2,1)} copy(bf16[64,2048]{1,0:T(8,128)(2,1)} %get-tuple-element.4) | data formatting | bytes 524288
  114.0 2.2 %copy.8 = bf16[1,256,1792]{2,1,0:T(8,128)(2,1)} copy(bf16[1,256,1792]{2,1,0:T(8,128)(2,1)} %get-tuple-element.5) | data formatting | bytes 1835008

commit v2 on v1

--- a/solution.py
+++ b/solution.py
@@ -13,7 +13,7 @@
 NX = NY = NL = 4
 NH = 2
 NZ = NH * NL
-TILE = 256
+TILE = 512
 
 
 class Ring:
@@ -59,7 +59,7 @@
 
 def kernel(
     acts_hbm, grad_hbm, w_hbm, gi_ref, gw_ref,
-    gp, gq, w, acts, xbuf, aall, at, acc, lhs, part, pair, near, mid,
+    gp, gq, w, acts, xbuf, aall, acc, lhs, part, pair, near, mid,
     ring_send, ring_recv, loc_sem, hx_send, hx_recv, ax_send, ax_recv, az_send, az_recv,
     ac_send, ac_recv, pr_send, pr_recv, rs_send, rs_recv,
 ):
@@ -158,6 +158,7 @@
     qb = [[q2(b, i) for i in ys] for b in (h, oh)]
 
     acc[...] = jnp.zeros_like(acc)
+    wide = acc.shape[1] // 2
 
     def group(is_p, b, i):
         if is_p:
@@ -166,12 +167,13 @@
         else:
             a = aall[1, b * NL + i].reshape(NX * half, kb)
             g = gq.at[b, i]
-        at[...] = a.astype(F32).T.astype(BF16)
-
-        @pl.loop(0, acc.shape[1] // TILE)
+
+        @pl.loop(0, acc.shape[1] // wide)
         def _(t):
-            n = pl.ds(pl.multiple_of(t * TILE, TILE), TILE)
-            acc[:, n] += jnp.dot(at[...], g[:, :, n].reshape(NX * half, TILE), preferred_element_type=F32)
+            n = pl.ds(pl.multiple_of(t * wide, 128), wide)
+            acc[:, n] += lax.dot_general(
+                a, g[:, :, n].reshape(NX * half, wide), (((0,), (0,)), ((), ())), preferred_element_type=F32
+            )
 
     def lr(r):
         r.from_left()
@@ -183,23 +185,21 @@
         first.from_right()
         second[2].own()
 
-    pa[0].own()
-    qa[0].own()
-    pb[0][0].own()
-    qb[0][0].own()
-
-    for cp in ax:
-        cp.wait_recv()
     az = []
-    for s in (1, NZ - 1, 2, NZ - 2, 3, NZ - 3, 4):
-        b = at_z(s) // NL
-        cp = pltpu.make_async_remote_copy(
-            xbuf.at[b], aall.at[c, z], az_send.at[s - 1], az_recv.at[s - 1],
-            device_id=dev_z(s), device_id_type=MESH,
-        )
-        cp.start()
-        az.append(cp)
-    aall[c, z] = xbuf[h]
+
+    def acts_z():
+        for cp in ax:
+            cp.wait_recv()
+        for s in (1, NZ - 1, 2, NZ - 2, 3, NZ - 3, 4):
+            b = at_z(s) // NL
+            cp = pltpu.make_async_remote_copy(
+                xbuf.at[b], aall.at[c, z], az_send.at[s - 1], az_recv.at[s - 1],
+                device_id=dev_z(s), device_id_type=MESH,
+            )
+            cp.start()
+            az.append(cp)
+        aall[c, z] = xbuf[h]
+        to_pal(0).start()
 
     def to_pal(s):
         ref = aall.at[c, at_z(s)]
@@ -213,54 +213,16 @@
             ref, ref, ac_send.at[s], ac_recv.at[s], device_id=pal, device_id_type=MESH
         )
 
-    to_pal(0).start()
-
-    grow(pa[0], pb[0])
-    grow(qa[0], qb[0])
-    lr(pb[0][0])
-    lr(qb[0][0])
-    pa[0].from_far()
-    pb[0][3].own()
-    qa[0].from_far()
-    qb[0][3].own()
-    for i in (1, 2):
-        lr(pb[0][i])
-        lr(qb[0][i])
-    hx_p.wait_recv()
-    pa[1].own()
-    pb[1][0].own()
-    hx_q.wait_recv()
-    qa[1].own()
-    qb[1][0].own()
-    lr(pb[0][3])
-    lr(qb[0][3])
-
-    for s in range(1, NZ):
-        ref = aall.at[c, at_z(NZ - s)]
-        pltpu.make_async_remote_copy(
-            ref, ref, az_send.at[s - 1], az_recv.at[s - 1], device_id=dev_z(s), device_id_type=MESH
-        ).wait_recv()
-        to_pal(NZ - s).start()
-
-    grow(pa[1], pb[1])
-    grow(qa[1], qb[1])
-    lr(pb[1][0])
-    lr(qb[1][0])
-    pa[1].from_far()
-    pb[1][3].own()
-    qa[1].from_far()
-    qb[1][3].own()
-
-    pb[0][0].from_far()
-    pb[1][0].from_far()
-    for d, s in enumerate((2, 0, 1, NZ - 1, NZ - 2)):
-        to = at_z(s)
-        lhs[0, d] = gp[to // NL, x, to % NL]
-        lhs[1, d] = gq[to // NL, to % NL, x]
-    own_w.wait()
-
-    def partial(k):
-        @pl.loop(0, nk // TILE)
+    def acts_core():
+        for s in range(1, NZ):
+            ref = aall.at[c, at_z(NZ - s)]
+            pltpu.make_async_remote_copy(
+                ref, ref, az_send.at[s - 1], az_recv.at[s - 1], device_id=dev_z(s), device_id_type=MESH
+            ).wait_recv()
+            to_pal(NZ - s).start()
+
+    def partial(k, lo, hi):
+        @pl.loop(lo, hi)
         def _(t):
             cols = pl.ds(pl.multiple_of(t * TILE, TILE), TILE)
             rows = pl.ds(pl.multiple_of(k * nk + t * TILE, TILE), TILE)
@@ -288,29 +250,78 @@
             out.append(cp)
         return out
 
-    partial(0)
+    def fill():
+
+        pb[0][0].from_far()
+        pb[1][0].from_far()
+        for d, s in enumerate((2, 0, 1, NZ - 1, NZ - 2)):
+            to = at_z(s)
+            lhs[0, d] = gp[to // NL, x, to % NL]
+            lhs[1, d] = gq[to // NL, to % NL, x]
+        own_w.wait()
+
+
+    pa[0].own()
+    qa[0].own()
+    pb[0][0].own()
+    qb[0][0].own()
+    pa[0].from_left()
+    pb[0][1].own()
+    qa[0].from_left()
+    qb[0][1].own()
+    pa[0].from_right()
+    qa[0].from_right()
+    lr(pb[0][0])
+    lr(qb[0][0])
+    qb[0][2].own()
+    hx_q.wait_recv()
+    qa[1].own()
+    qb[1][0].own()
+    hx_p.wait_recv()
+    pb[1][0].own()
+    pa[1].own()
+    acts_z()
+    lr(qb[0][1])
+    pa[0].from_far()
+    lr(qa[1])
+    lr(pb[1][0])
+    pb[0][2].own()
+    lr(pb[0][1])
+    qa[0].from_far()
+    qb[0][3].own()
+    pb[0][3].own()
+    qb[1][1].own()
+    qb[1][2].own()
+    lr(qb[0][2])
+    qa[1].from_far()
+    fill()
+    qb[1][3].own()
+    partial(0, 0, nk // TILE)
     pair_copy(0).start()
-    lr(pb[1][1])
-    lr(qb[1][1])
+    grow(pa[1], pb[1])
+    partial(1, 0, nk // TILE // 2)
     rs = scatter(0)
-    partial(1)
+    partial(1, nk // TILE // 2, nk // TILE)
     pair_copy(1).start()
-    lr(pb[1][2])
-    lr(qb[1][2])
+    lr(qb[1][0])
+    lr(pb[0][2])
+    pa[1].from_far()
+    pb[1][3].own()
     rs += scatter(1)
-
+    lr(pb[0][3])
+    lr(qb[0][3])
+    acts_core()
     for s in range(NZ):
         from_pal(s).wait_recv()
-    for i in range(1, 4):
-        pb[0][i].from_far()
     for i in range(4):
+        if i:
+            pb[0][i].from_far()
         qb[0][i].from_far()
         group(True, h, xs[i])
-        if i == 1:
-            lr(pb[1][3])
-            lr(qb[1][3])
-    for i in range(4):
         group(False, h, ys[i])
+        if i < 3:
+            lr(pb[1][1 + i])
+            lr(qb[1][1 + i])
     for i in range(4):
         if i:
             pb[1][i].from_far()
@@ -356,7 +367,6 @@
             pltpu.VMEM((frames, width), BF16),
             pltpu.VMEM((NH, NX, frames, kb), BF16),
             pltpu.VMEM((2, NZ, NX, frames, kb), BF16),
-            pltpu.VMEM((kb, NX * half), BF16),
             pltpu.VMEM((kb, hidden), F32),
             pltpu.VMEM((2, 5, half, hidden), BF16),
             pltpu.VMEM((2, 2, 4, half, nk), F32),

time: 117 us -> 102 us (0.87)
  Pallas kernels: 112 us -> 97.1 us
    pallas_call x1, Pallas kernels: 112 us -> 97.1 us  [shards(): pl.pallas_call(kernel, out_shape=(jax.ShapeDtypeStruct((frames, width), B...]
where the time goes in v2:
time: 102 us
  Pallas kernels  97.1 us (95%)
  local copies, waits for them, and re-layouts  3.83 us (4%)
    pallas_call x1, Pallas kernels, shards(): pl.pallas_call(kernel, out_shape=(jax.ShapeDtypeStruct((frames, width), B...  97.1 us
    unnamed x2, local copies, waits for them, and re-layouts  3.83 us

profile of v2, /device:TPU:1, one launch (start us, length us, event | category | flops | bytes accessed | tf_op | source)
XLA Modules:
  0.0 101.6 jit_solution(15589129258840617213)
XLA Ops:
  0.6 97.1 %grads.1 = (bf16[64,2048]{1,0:T(8,128)(2,1)}, bf16[1,256,1792]{2,1,0:T(8,128)(2,1)}) custom-call(bf16[64,2048]{1,0:T(8,128)(2,1)} %acts_hbm.1, bf16[128,1792]{1,0:T(8,128)(2,1)} %grad_hbm.1, bf16[2048,1792]{1,0:T(8,128)(2,1)} %w_hbm.1), custom_call_target="tpu_custom_call" | custom-call | tf_op jit(solution)/shard_map/grads/pallas_call | solution.py:355
  97.7 1.7 %copy.7 = bf16[64,2048]{1,0:T(8,128)(2,1)} copy(bf16[64,2048]{1,0:T(8,128)(2,1)} %get-tuple-element.4) | data formatting | bytes 524288
  99.4 2.2 %copy.8 = bf16[1,256,1792]{2,1,0:T(8,128)(2,1)} copy(bf16[1,256,1792]{2,1,0:T(8,128)(2,1)} %get-tuple-element.5) | data formatting | bytes 1835008

commit v3 on v2

--- a/solution.py
+++ b/solution.py
@@ -175,16 +175,6 @@
                 a, g[:, :, n].reshape(NX * half, wide), (((0,), (0,)), ((), ())), preferred_element_type=F32
             )
 
-    def lr(r):
-        r.from_left()
-        r.from_right()
-
-    def grow(first, second):
-        first.from_left()
-        second[1].own()
-        first.from_right()
-        second[2].own()
-
     az = []
 
     def acts_z():
@@ -251,83 +241,122 @@
         return out
 
     def fill():
-
-        pb[0][0].from_far()
-        pb[1][0].from_far()
         for d, s in enumerate((2, 0, 1, NZ - 1, NZ - 2)):
             to = at_z(s)
             lhs[0, d] = gp[to // NL, x, to % NL]
             lhs[1, d] = gq[to // NL, to % NL, x]
         own_w.wait()
 
-
+    rs = []
+    pb[0][0].own()
     pa[0].own()
+    qb[0][0].own()
     qa[0].own()
-    pb[0][0].own()
-    qb[0][0].own()
+    pa[0].from_right()
     pa[0].from_left()
+    pb[0][2].own()
+    qa[0].from_right()
+    qb[0][2].own()
     pb[0][1].own()
     qa[0].from_left()
-    qb[0][1].own()
-    pa[0].from_right()
-    qa[0].from_right()
-    lr(pb[0][0])
-    lr(qb[0][0])
-    qb[0][2].own()
-    hx_q.wait_recv()
-    qa[1].own()
-    qb[1][0].own()
     hx_p.wait_recv()
     pb[1][0].own()
+    pb[0][0].from_left()
     pa[1].own()
-    acts_z()
-    lr(qb[0][1])
-    pa[0].from_far()
-    lr(qa[1])
-    lr(pb[1][0])
-    pb[0][2].own()
-    lr(pb[0][1])
+    pb[0][2].from_left()
+    qb[0][1].own()
+    qb[0][2].from_right()
+    pb[0][1].from_right()
     qa[0].from_far()
     qb[0][3].own()
+    acts_z()
+    qb[0][2].from_left()
+    pb[0][0].from_right()
+    pa[1].from_right()
+    hx_q.wait_recv()
+    qb[0][1].from_left()
+    qb[1][0].own()
+    qa[1].own()
+    pb[1][0].from_right()
+    qb[0][0].from_right()
+    pb[0][0].from_far()
+    qb[0][1].from_right()
+    qb[0][3].from_left()
+    pb[1][0].from_left()
+    pa[0].from_far()
+    qb[0][3].from_right()
+    pa[1].from_left()
+    qa[1].from_left()
+    qa[1].from_right()
+    pb[1][1].own()
+    qb[1][2].own()
+    pb[0][2].from_right()
+    pb[1][0].from_far()
+    qb[0][0].from_left()
+    pb[1][2].own()
     pb[0][3].own()
-    qb[1][1].own()
-    qb[1][2].own()
-    lr(qb[0][2])
     qa[1].from_far()
     fill()
+    qb[1][0].from_left()
+    partial(1, 0, nk // TILE)
+    pair_copy(1).start()
+    qb[1][0].from_right()
     qb[1][3].own()
+    rs += scatter(1)
+    qb[0][3].from_far()
+    qb[0][2].from_far()
     partial(0, 0, nk // TILE)
     pair_copy(0).start()
-    grow(pa[1], pb[1])
-    partial(1, 0, nk // TILE // 2)
-    rs = scatter(0)
-    partial(1, nk // TILE // 2, nk // TILE)
-    pair_copy(1).start()
-    lr(qb[1][0])
-    lr(pb[0][2])
+    acts_core()
+    pb[0][1].from_left()
+    qb[1][1].own()
+    pb[1][2].from_right()
     pa[1].from_far()
     pb[1][3].own()
-    rs += scatter(1)
-    lr(pb[0][3])
-    lr(qb[0][3])
-    acts_core()
+    pb[1][2].from_left()
     for s in range(NZ):
         from_pal(s).wait_recv()
-    for i in range(4):
-        if i:
-            pb[0][i].from_far()
-        qb[0][i].from_far()
-        group(True, h, xs[i])
-        group(False, h, ys[i])
-        if i < 3:
-            lr(pb[1][1 + i])
-            lr(qb[1][1 + i])
-    for i in range(4):
-        if i:
-            pb[1][i].from_far()
-        group(True, oh, xs[i])
-        qb[1][i].from_far()
-        group(False, oh, ys[i])
+    qb[1][0].from_far()
+    group(True, h, xs[0])
+    pb[0][3].from_right()
+    qb[0][0].from_far()
+    pb[0][2].from_far()
+    qb[0][1].from_far()
+    qb[1][2].from_left()
+    group(True, oh, xs[0])
+    rs += scatter(0)
+    group(False, h, ys[2])
+    pb[0][3].from_left()
+    qb[1][2].from_right()
+    group(False, h, ys[1])
+    pb[0][1].from_far()
+    group(False, oh, ys[0])
+    pb[1][1].from_right()
+    qb[1][3].from_right()
+    group(False, h, ys[0])
+    pb[1][1].from_left()
+    pb[1][3].from_left()
+    qb[1][3].from_left()
+    group(False, h, ys[3])
+    group(True, h, xs[2])
+    qb[1][1].from_left()
+    pb[1][3].from_right()
+    qb[1][1].from_right()
+    pb[1][2].from_far()
+    pb[0][3].from_far()
+    group(True, h, xs[3])
+    qb[1][2].from_far()
+    group(True, oh, xs[2])
+    group(False, oh, ys[2])
+    group(True, h, xs[1])
+    qb[1][3].from_far()
+    group(False, oh, ys[3])
+    pb[1][1].from_far()
+    group(True, oh, xs[1])
+    pb[1][3].from_far()
+    group(True, oh, xs[3])
+    qb[1][1].from_far()
+    group(False, oh, ys[1])
 
     for cp in rs:
         cp.wait_recv()
@@ -345,6 +374,19 @@
     pair_copy(1).wait_send()
 
 
+def finish(gi_in, gw_in, gi_out, gw_out, gi_buf, gw_buf, sems):
+    pairs = ((gw_in, gw_buf, gw_out), (gi_in, gi_buf, gi_out))
+    into = [pltpu.make_async_copy(a, b, sems.at[k, 0]) for k, (a, b, _) in enumerate(pairs)]
+    outof = [pltpu.make_async_copy(b, o, sems.at[k, 1]) for k, (_, b, o) in enumerate(pairs)]
+    for cp in into:
+        cp.start()
+    for cp, out in zip(into, outof):
+        cp.wait()
+        out.start()
+    for out in outof:
+        out.wait()
+
+
 def shards(acts, grad_out, weight):
     frames, width = acts.shape
     rows, hidden = grad_out.shape
@@ -352,7 +394,7 @@
     kb = width // NZ
     nk = width // 2
     dma = pltpu.SemaphoreType.DMA
-    return pl.pallas_call(
+    gi, gw = pl.pallas_call(
         kernel,
         out_shape=(
             jax.ShapeDtypeStruct((frames, width), BF16),
@@ -381,6 +423,14 @@
         ),
         name="grads",
     )(acts, grad_out, weight)
+    return pl.pallas_call(
+        finish,
+        out_shape=(jax.ShapeDtypeStruct(gi.shape, BF16), jax.ShapeDtypeStruct(gw.shape, BF16)),
+        in_specs=[pl.BlockSpec(memory_space=pl.ANY)] * 2,
+        out_specs=(pl.BlockSpec(memory_space=pl.ANY),) * 2,
+        scratch_shapes=[pltpu.VMEM(gi.shape, BF16), pltpu.VMEM(gw.shape, BF16), dma((2, 2))],
+        name="finish",
+    )(gi, gw)
 
 
 def solution(mesh):

time: 102 us -> 96.2 us (0.943)
  local copies, waits for them, and re-layouts: 3.83 us -> 0 us
  Pallas kernels: 97.1 us -> 95.4 us
    pallas_call x1, Pallas kernels: 97.1 us -> 93.2 us  [shards(): pl.pallas_call(kernel, out_shape=(jax.ShapeDtypeStruct((frames, width), B...]
    unnamed x2 -> x0, local copies, waits for them, and re-layouts: 3.83 us -> none
    pallas_call x0 -> x1, Pallas kernels: none -> 2.22 us  [shards(): pl.pallas_call(finish, out_shape=(jax.ShapeDtypeStruct(gi.shape, BF16), j...]
where the time goes in v3:
time: 96.2 us; the launch traced here: 96 us
  Pallas kernels  95.4 us (99%)
    pallas_call x1, Pallas kernels, shards(): pl.pallas_call(kernel, out_shape=(jax.ShapeDtypeStruct((frames, width), B...  93.2 us
    pallas_call x1, Pallas kernels, shards(): pl.pallas_call(finish, out_shape=(jax.ShapeDtypeStruct(gi.shape, BF16), j...  2.22 us

profile of v3, /device:TPU:1, one launch (start us, length us, event | category | flops | bytes accessed | tf_op | source)
XLA Modules:
  0.0 96.0 jit_solution(4859786654816641632)
XLA Ops:
  0.6 93.2 %grads.1 = (bf16[64,2048]{1,0:T(8,128)(2,1)}, bf16[1,256,1792]{2,1,0:T(8,128)(2,1)}) custom-call(bf16[64,2048]{1,0:T(8,128)(2,1)} %acts_hbm.1, bf16[128,1792]{1,0:T(8,128)(2,1)} %grad_hbm.1, bf16[2048,1792]{1,0:T(8,128)(2,1)} %w_hbm.1), custom_call_target="tpu_custom_call" | custom-call | tf_op jit(solution)/shard_map/grads/pallas_call | solution.py:397
  93.8 2.2 %finish.1 = (bf16[64,2048]{1,0:T(8,128)(2,1)}, bf16[1,256,1792]{2,1,0:T(8,128)(2,1)}) custom-call(bf16[64,2048]{1,0:T(8,128)(2,1)} %get-tuple-element.4.gi_in, bf16[1,256,1792]{2,1,0:T(8,128)(2,1)} %get-tuple-element.5.gw_in), custom_call_target="tpu_custom_call" | custom-call | tf_op jit(solution)/shard_map/finish/pallas_call | solution.py:426

commit v4 on v0

v4 whole, which is shorter than its diff:
```python
import functools

import jax
import jax.numpy as jnp
from jax import lax
from jax.experimental import pallas as pl
from jax.experimental.pallas import tpu as pltpu
from jax.sharding import PartitionSpec as P

MESH = pl.DeviceIdType.MESH
F32 = jnp.float32
BF16 = jnp.bfloat16
NX = NY = NL = 4
NH = 2
NZ = NH * NL
TILE = 512


def chunks_of(hidden):
    return [(a * hidden // 14, n * hidden // 14) for a, n in ((0, 3), (3, 4), (7, 4), (11, 3))]


class Ring:
    def __init__(self, slot, loc, me, n, dev, send_sem, recv_sem):
        self.slot, self.loc, self.dev = slot, loc, dev
        self.me = me
        self.left, self.right, self.far = (lax.rem(me + s, n) for s in (n - 1, 1, 2))
        self.sends, self.recvs = send_sem, recv_sem

    def _copy(self, ref, k, to):
        i = self.slot * 4 + k
        return pltpu.make_async_remote_copy(
            ref, ref, self.sends.at[i], self.recvs.at[i], device_id=self.dev(to), device_id_type=MESH
        )

    def _half(self, o, k):
        ref = self.loc(o)
        rows = ref.shape[0] // 2
        return ref.at[pl.ds(k * rows, rows)]

    def own(self):
        self._copy(self.loc(self.me), 0, self.right).start()
        self._copy(self.loc(self.me), 1, self.left).start()

    def from_left(self):
        self._copy(self.loc(self.left), 0, self.right).wait_recv()
        self._copy(self._half(self.left, 0), 2, self.right).start()

    def from_right(self):
        self._copy(self.loc(self.right), 1, self.left).wait_recv()
        self._copy(self._half(self.right, 1), 3, self.left).start()

    def from_far(self):
        self._copy(self._half(self.far, 0), 2, self.right).wait_recv()
        self._copy(self._half(self.far, 1), 3, self.left).wait_recv()

    def wait_sent(self):
        self._copy(self.loc(self.me), 0, self.right).wait_send()
        self._copy(self.loc(self.me), 1, self.left).wait_send()
        self._copy(self._half(self.left, 0), 2, self.right).wait_send()
        self._copy(self._half(self.right, 1), 3, self.left).wait_send()


def kernel(
    acts_hbm, grad_hbm, w_hbm, gi_ref, gw_ref,
    gp, gq, w, acts, xbuf, aall, acc, wsend, wrecv, lhs, part, pair, near, mid,
    ring_send, ring_recv, pa_send, pa_recv, loc_sem, hx_send, hx_recv, ax_send, ax_recv, az_send, az_recv,
    ac_send, ac_recv, pr_send, pr_recv, rs_send, rs_recv, ws_send, ws_recv,
):
    dp, y, col = lax.axis_index("dp"), lax.axis_index("row"), lax.axis_index("col")
    h, x, l, c = dp // NX, dp % NX, col // 2, col % 2
    z = h * NL + l
    odd = x % 2
    px = x + 1 - 2 * odd
    bx = (x + 2 * odd + NX - 1) % NX
    pbx = (px + 2 - 2 * odd + NX - 1) % NX
    half = gp.shape[3]
    kb = acts.shape[1] // NZ
    nk = part.shape[4]
    cuts = chunks_of(gp.shape[4])
    nj = len(cuts)

    def dev_x(to):
        return (h * NX + to, y, col)

    def dev_y(to):
        return (dp, to, col)

    def at_z(s):
        return lax.rem(z + s, NZ)

    def dev_z(s):
        to = at_z(s)
        return ((to // NL) * NX + x, y, (to % NL) * 2 + c)

    def side(to):
        return (to // NL + h) % 2

    pal = (dp, y, l * 2 + 1 - c)

    own_p = pltpu.make_async_copy(grad_hbm.at[pl.ds(0, half)], gp.at[0, 0, y], loc_sem.at[0])
    own_q = pltpu.make_async_copy(grad_hbm.at[pl.ds(half, half)], gq.at[0, 0, y], loc_sem.at[1])
    own_a = pltpu.make_async_copy(acts_hbm, acts, loc_sem.at[2])
    own_w = pltpu.make_async_copy(w_hbm, w, loc_sem.at[3])
    own_a.start()
    own_p.start()
    own_q.start()
    own_w.start()

    barrier = pltpu.get_barrier_semaphore()
    peers = [dev_x(px), dev_x(bx)] + [dev_y(lax.rem(y + s, NY)) for s in (1, NY - 1)]
    peers += [dev_z(s) for s in range(1, NZ)] + [pal]
    for peer in peers:
        pl.semaphore_signal(barrier, inc=1, device_id=peer, device_id_type=MESH)
    own_a.wait()
    own_p.wait()
    own_q.wait()
    pl.semaphore_wait(barrier, len(peers))

    def remote(src, dst, send, recv, i, to):
        return pltpu.make_async_remote_copy(
            src, dst, send.at[i], recv.at[i], device_id=to, device_id_type=MESH
        )

    def lanes(j):
        return pl.ds(cuts[j][0], cuts[j][1])

    class Chunk:
        def __init__(self, b, j):
            self.b, self.j, self.i = b, j, b * nj + j
            n = lanes(j)

            def ring(k, ref, s):
                return Ring(
                    k * NH * nj + self.i, lambda o: ref.at[b, s, o, :, n], y, NY, dev_y, ring_send, ring_recv
                )

            self.yq, self.y0, self.y1 = ring(0, gq, 0), ring(1, gp, 0), ring(2, gp, 1)
            self.pa = remote(
                gp.at[b, 0, y, :, n], gp.at[b, 1, y, :, n], pa_send, pa_recv, self.i * 5 + 4, dev_x(px)
            )
            self.qa = [
                remote(gq.at[b, 0, o, :, n], gq.at[b, 1, o, :, n], pa_send, pa_recv, self.i * 5 + k, dev_x(px))
                for k, o in enumerate(lax.rem(y + s, NY) for s in (0, NY - 1, 1, 2))
            ]
            self.hx = [
                remote(ref.at[0, 0, y, :, n], ref.at[1, 0, y, :, n], hx_send, hx_recv, j * 2 + k, dev_z(NL))
                for k, ref in enumerate((gp, gq))
            ]

        def byq(self):
            if self.b:
                self.hx[1].wait_recv()
            self.yq.own()

        def by0(self):
            if self.b:
                self.hx[0].wait_recv()
            self.y0.own()

        def bpa(self):
            self.pa.start()

        def bqa(self):
            self.qa[0].start()

        def mql(self):
            self.yq.from_left()
            self.qa[1].start()

        def mqr(self):
            self.yq.from_right()
            self.qa[2].start()

        def m0(self):
            self.y0.from_left()
            self.y0.from_right()

        def mp(self):
            self.pa.wait_recv()
            self.y1.own()

        def eq(self):
            self.yq.from_far()
            self.qa[3].start()

        def ep(self):
            self.y1.from_left()
            self.y1.from_right()

        def e0(self):
            self.y0.from_far()

        def dn(self):
            self.y1.from_far()
            for q in self.qa:
                q.wait_recv()

        def wait_sent(self):
            for r in (self.yq, self.y0, self.y1):
                r.wait_sent()
            for cp in self.qa + [self.pa]:
                cp.wait_send()
            if not self.b:
                for cp in self.hx:
                    cp.wait_send()

    ch = [[Chunk(b, j) for j in range(nj)] for b in range(NH)]

    ax = []
    for b in range(NH):
        for r, (theirs, mine) in enumerate(((pbx, bx), (px, x))):
            cols = pl.ds(pl.multiple_of((b * NX + theirs) * kb, kb), kb)
            ax.append(remote(acts.at[:, cols], xbuf.at[b, r, 1], ax_send, ax_recv, b * 2 + r, dev_x(px)))
            ax[-1].start()
            cols = pl.ds(pl.multiple_of((b * NX + mine) * kb, kb), kb)
            xbuf[b, r, 0] = acts[:, cols]

    def az(r, s, to):
        b = at_z(s) // NL
        return remote(
            xbuf.at[b, r], aall.at[r, c, side(to), :, to % NL], az_send, az_recv, r * NZ + s, dev_z(s)
        )

    def acts_z(r):
        for s in (1, NZ - 1, 2, NZ - 2, 3, NZ - 3, 4):
            b = at_z(s) // NL
            remote(
                xbuf.at[b, r], aall.at[r, c, (b + h) % 2, :, l], az_send, az_recv, r * NZ + s, dev_z(s)
            ).start()
        aall[r, c, 0, :, l] = xbuf[h, r]

    def ac(r, cc):
        return remote(aall.at[r, cc], aall.at[r, cc], ac_send, ac_recv, r, pal)

    def acts_core(r):
        for s in range(1, NZ):
            az(r, s, at_z(NZ - s)).wait_recv()
        ac(r, c).start()

    def wgrad(r, j):
        n = lanes(j)
        out = None
        for cc, g in enumerate((gp, gq)):
            t = lax.dot_general(
                aall[r, cc].reshape(-1, kb), g[:, :, :, :, n].reshape(-1, cuts[j][1]),
                (((0,), (0,)), ((), ())), preferred_element_type=F32,
            )
            out = t if out is None else out + t
        if r:
            acc[:, n] = out
        else:
            wsend[:, n] = out

    def ws(j):
        return remote(wsend.at[:, lanes(j)], wrecv.at[:, lanes(j)], ws_send, ws_recv, j, dev_x(bx))

    def fill():
        for d, s in enumerate((2, 0, 1, NZ - 1, NZ - 2)):
            to = at_z(s)
            lhs[0, d] = gp[side(to), 0, to % NL]
            lhs[1, d] = gq[side(to), 0, to % NL]

    def partial(k, lo, hi):
        @pl.loop(lo, hi)
        def _(t):
            cols = pl.ds(pl.multiple_of(t * TILE, TILE), TILE)
            rows = pl.ds(pl.multiple_of(k * nk + t * TILE, TILE), TILE)
            both = lhs[:, k : k + 4].reshape(8 * half, lhs.shape[3])
            r = lax.dot_general(both, w[rows], (((1,), (1,)), ((), ())), preferred_element_type=F32)
            part[:, k, :, :, cols] = r.reshape(2, 4, half, TILE)

    def pair_copy(k):
        return remote(part.at[1 - c, k], pair.at[k], pr_send, pr_recv, k, pal)

    def scatter(k):
        pair_copy(k).wait_recv()
        part[c, k] += pair[k]
        todo = (((0, 2, mid.at[0]), (2, 1, near.at[0, 0]), (3, NZ - 1, near.at[1, 0])) if k == 0 else
                ((3, NZ - 2, mid.at[1]), (1, 1, near.at[0, 1]), (2, NZ - 1, near.at[1, 1])))
        out = []
        for i, (d, s, dst) in enumerate(todo):
            out.append(remote(part.at[c, k, d], dst, rs_send, rs_recv, k * 3 + i, dev_z(s)))
            out[-1].start()
        return out

    def hx(j):
        for cp in ch[0][j].hx:
            cp.start()

    rs = []
    hx(3)
    ch[0][3].by0()
    ch[0][2].byq()
    ch[0][0].byq()
    hx(2)
    ch[0][2].bqa()
    ch[0][2].by0()
    ch[0][3].byq()
    ch[0][1].byq()
    hx(0)
    ch[0][2].bpa()
    ch[0][0].bqa()
    for cp in ax:
        cp.wait_recv()
    ch[0][2].mql()
    ch[1][3].byq()
    ch[0][0].bpa()
    ch[0][1].bpa()
    ch[0][2].m0()
    ch[0][3].mqr()
    ch[0][0].by0()
    ch[0][2].mqr()
    ch[1][3].mqr()
    ch[1][3].by0()
    ch[1][3].bqa()
    ch[1][2].byq()
    ch[0][2].mp()
    ch[0][0].mql()
    ch[0][3].bpa()
    ch[1][3].bpa()
    ch[0][2].e0()
    ch[1][3].m0()
    ch[1][2].by0()
    ch[0][1].by0()
    ch[1][2].bpa()
    acts_z(0)
    ch[1][2].mql()
    ch[0][0].mqr()
    ch[0][2].ep()
    ch[1][2].bqa()
    ch[0][2].eq()
    ch[1][0].byq()
    ch[1][3].mql()
    ch[1][2].mqr()
    ch[1][0].by0()
    ch[1][2].m0()
    ch[1][0].mqr()
    ch[1][2].mp()
    ch[0][0].m0()
    ch[1][0].m0()
    ch[0][1].m0()
    ch[1][0].bpa()
    ch[1][2].eq()
    ch[0][1].mqr()
    ch[1][0].mql()
    hx(1)
    ch[1][2].ep()
    ch[0][3].mp()
    ch[0][0].mp()
    ch[0][3].mql()
    ch[0][1].mql()
    ch[1][2].e0()
    ch[0][0].e0()
    ch[0][1].mp()
    acts_core(0)
    ch[1][0].mp()
    ch[1][0].eq()
    ch[1][0].bqa()
    ch[0][3].m0()
    ch[0][3].ep()
    ch[0][0].eq()
    ch[1][2].dn()
    ch[0][0].ep()
    ch[1][3].mp()
    ch[0][3].eq()
    ch[1][3].e0()
    ac(0, 1 - c).wait_recv()
    ch[0][2].dn()
    ch[1][0].e0()
    wgrad(0, 2)
    ws(2).start()
    ch[1][0].ep()
    ch[1][1].byq()
    acts_z(1)
    ch[1][1].by0()
    ch[0][1].bqa()
    ch[0][1].eq()
    ch[1][1].mql()
    ch[0][0].dn()
    ch[1][1].bpa()
    ch[1][1].mqr()
    ch[0][3].e0()
    ch[1][1].m0()
    ch[1][0].dn()
    ch[1][3].ep()
    wgrad(0, 0)
    ws(0).start()
    ch[0][1].e0()
    ch[1][1].eq()
    ch[0][3].bqa()
    ch[1][1].bqa()
    ch[1][3].eq()
    ch[0][1].ep()
    ch[1][1].e0()
    own_w.wait()
    fill()
    partial(1, 0, nk // TILE)
    pair_copy(1).start()
    partial(0, 0, nk // TILE)
    pair_copy(0).start()
    rs += scatter(1)
    ch[1][3].dn()
    ch[1][1].mp()
    acts_core(1)
    ch[0][3].dn()
    wgrad(0, 3)
    ws(3).start()
    ch[0][1].dn()
    ch[1][1].ep()
    ch[1][1].dn()
    wgrad(0, 1)
    ws(1).start()
    rs += scatter(0)
    ac(1, 1 - c).wait_recv()
    wgrad(1, 1)
    wgrad(1, 3)
    wgrad(1, 0)
    wgrad(1, 2)

    for j in range(nj):
        ws(j).wait_recv()
        n = lanes(j)
        gw_ref[0, :, n] = (acc[:, n] + wrecv[:, n]).astype(BF16)
    for cp in rs:
        cp.wait_recv()
    gi_ref[:, :nk] = (part[c, 0, 1] + mid[0] + near[0, 0] + near[1, 0]).astype(BF16)
    gi_ref[:, nk:] = (part[c, 1, 0] + mid[1] + near[0, 1] + near[1, 1]).astype(BF16)

    for b in range(NH):
        for j in range(nj):
            ch[b][j].wait_sent()
    for r in range(2):
        for s in range(1, NZ):
            az(r, s, z).wait_send()
        ac(r, c).wait_send()
    for j in range(nj):
        ws(j).wait_send()
    for cp in ax + rs:
        cp.wait_send()
    pair_copy(0).wait_send()
    pair_copy(1).wait_send()


def finish(gi_in, gw_in, gi_out, gw_out, gi_buf, gw_buf, sems):
    pairs = ((gw_in, gw_buf, gw_out), (gi_in, gi_buf, gi_out))
    into = [pltpu.make_async_copy(a, b, sems.at[k, 0]) for k, (a, b, _) in enumerate(pairs)]
    outof = [pltpu.make_async_copy(b, o, sems.at[k, 1]) for k, (_, b, o) in enumerate(pairs)]
    for cp in into:
        cp.start()
    for cp, out in zip(into, outof):
        cp.wait()
        out.start()
    for out in outof:
        out.wait()


def shards(acts, grad_out, weight):
    frames, width = acts.shape
    rows, hidden = grad_out.shape
    half = rows // 2
    kb = width // NZ
    nk = width // 2
    nj = len(chunks_of(hidden))
    dma = pltpu.SemaphoreType.DMA
    counts = [3 * NH * nj * 4] * 2 + [5 * NH * nj] * 2 + [4] + [2 * nj] * 2 + [4] * 2 + [2 * NZ] * 2
    counts += [2] * 2 + [2] * 2 + [6] * 2 + [nj] * 2
    gi, gw = pl.pallas_call(
        kernel,
        out_shape=(
            jax.ShapeDtypeStruct((frames, width), BF16),
            jax.ShapeDtypeStruct((1, kb, hidden), BF16),
        ),
        in_specs=[pl.BlockSpec(memory_space=pl.ANY)] * 3,
        out_specs=(pl.BlockSpec(memory_space=pltpu.VMEM),) * 2,
        scratch_shapes=[
            pltpu.VMEM((NH, 2, NY, half, hidden), BF16),
            pltpu.VMEM((NH, 2, NY, half, hidden), BF16),
            pltpu.VMEM((width, hidden), BF16),
            pltpu.VMEM((frames, width), BF16),
            pltpu.VMEM((NH, 2, 2, frames, kb), BF16),
            pltpu.VMEM((2, 2, NH, 2, NL, frames, kb), BF16),
            pltpu.VMEM((kb, hidden), F32),
            pltpu.VMEM((kb, hidden), F32),
            pltpu.VMEM((kb, hidden), F32),
            pltpu.VMEM((2, 5, half, hidden), BF16),
            pltpu.VMEM((2, 2, 4, half, nk), F32),
            pltpu.VMEM((2, 4, half, nk), F32),
            pltpu.VMEM((2, 2, half, nk), F32),
            pltpu.VMEM((2, half, nk), F32),
        ]
        + [dma((n,)) for n in counts],
        compiler_params=pltpu.CompilerParams(
            collective_id=0, has_side_effects=True, vmem_limit_bytes=62 << 20
        ),
        name="grads",
    )(acts, grad_out, weight)
    return pl.pallas_call(
        finish,
        out_shape=(jax.ShapeDtypeStruct(gi.shape, BF16), jax.ShapeDtypeStruct(gw.shape, BF16)),
        in_specs=[pl.BlockSpec(memory_space=pl.ANY)] * 2,
        out_specs=(pl.BlockSpec(memory_space=pl.ANY),) * 2,
        scratch_shapes=[pltpu.VMEM(gi.shape, BF16), pltpu.VMEM(gw.shape, BF16), dma((2, 2))],
        name="finish",
    )(gi, gw)


def solution(mesh):
    in_specs = (P(("dp", "col"), "row"), P(("dp", "row"), "col"), P("row", "col"))
    out_specs = (P(("dp", "col"), "row"), P("row", "dp", "col"))
    return jax.shard_map(shards, mesh=mesh, in_specs=in_specs, out_specs=out_specs, check_vma=False)
```

time: 421 us -> 94.8 us (0.23)
  waiting for transfers between devices: 311 us -> 0 us
  Pallas kernels: 0 us -> 93 us
  blocking collectives: 70.2 us -> 0 us
  matrix products: 17.9 us -> 0 us
  between operations: 13.8 us -> 0.64 us
  local copies, waits for them, and re-layouts: 5.72 us -> 0 us
    all_gather x3 -> x0, waiting for transfers between devices: 289 us -> none  [the longest x1 224 us: shards(): lax.all_gather(grad_out, ('dp', 'row'), axis=0, tiled=True)]
    pallas_call x0 -> x2, Pallas kernels: none -> 93 us  [the longest x1 90.8 us: shards(): pl.pallas_call(kernel, out_shape=(jax.ShapeDtypeStruct((frames, width), B...]
    all_to_all x1 -> x0, blocking collectives: 70.2 us -> none  [shards(): lax.all_to_all(act_local, 'dp', split_axis=1, concat_axis=0, tiled=True)]
    reduce_scatter x1 -> x0, waiting for transfers between devices: 20.1 us -> none  [shards(): lax.psum_scatter(partial_value, 'col', scatter_dimension=0, tiled=True)]
    dot_general x2 -> x0, matrix products: 17.9 us -> none  [the longest x1 9.6 us: shards(): lax.dot_general(lax.all_gather(grad_out, 'row', axis=0, tiled=True), weig...]
  transfers between devices with their start and end apart: 4 -> 0, of which waited for: 4 -> 0; matrix products, arithmetic and copies ran while one was open for 4% -> 0% of each run, Pallas kernels for 0% -> 0%
where the time goes in v4:
time: 94.8 us; the launch traced here: 93.7 us
  Pallas kernels  93 us (98%)
    pallas_call x1, Pallas kernels, shards(): pl.pallas_call(kernel, out_shape=(jax.ShapeDtypeStruct((frames, width), B...  90.8 us
    pallas_call x1, Pallas kernels, shards(): pl.pallas_call(finish, out_shape=(jax.ShapeDtypeStruct(gi.shape, BF16), j...  2.22 us

profile of v4, /device:TPU:1, one launch (start us, length us, event | category | flops | bytes accessed | tf_op | source)
XLA Modules:
  0.0 93.7 jit_solution(10750297973599718102)
XLA Ops:
  0.6 90.8 %grads.1 = (bf16[64,2048]{1,0:T(8,128)(2,1)}, bf16[1,256,1792]{2,1,0:T(8,128)(2,1)}) custom-call(bf16[64,2048]{1,0:T(8,128)(2,1)} %acts_hbm.1, bf16[128,1792]{1,0:T(8,128)(2,1)} %grad_hbm.1, bf16[2048,1792]{1,0:T(8,128)(2,1)} %w_hbm.1), custom_call_target="tpu_custom_call" | custom-call | tf_op jit(solution)/shard_map/grads/pallas_call | solution.py:468
  91.4 2.2 %finish.1 = (bf16[64,2048]{1,0:T(8,128)(2,1)}, bf16[1,256,1792]{2,1,0:T(8,128)(2,1)}) custom-call(bf16[64,2048]{1,0:T(8,128)(2,1)} %get-tuple-element.4.gi_in, bf16[1,256,1792]{2,1,0:T(8,128)(2,1)} %get-tuple-element.5.gw_in), custom_call_target="tpu_custom_call" | custom-call | tf_op jit(solution)/shard_map/finish/pallas_call | solution.py:498

commit v5 on v4

--- a/solution.py
+++ b/solution.py
@@ -280,8 +280,8 @@
                 ((3, NZ - 2, mid.at[1]), (1, 1, near.at[0, 1]), (2, NZ - 1, near.at[1, 1])))
         out = []
         for i, (d, s, dst) in enumerate(todo):
-            out.append(remote(part.at[c, k, d], dst, rs_send, rs_recv, k * 3 + i, dev_z(s)))
-            out[-1].start()
+            out.append((k, remote(part.at[c, k, d], dst, rs_send, rs_recv, k * 3 + i, dev_z(s))))
+            out[-1][1].start()
         return out
 
     def hx(j):
@@ -418,14 +418,24 @@
     wgrad(1, 0)
     wgrad(1, 2)
 
-    for j in range(nj):
+    def gw_piece(j):
         ws(j).wait_recv()
         n = lanes(j)
         gw_ref[0, :, n] = (acc[:, n] + wrecv[:, n]).astype(BF16)
-    for cp in rs:
-        cp.wait_recv()
-    gi_ref[:, :nk] = (part[c, 0, 1] + mid[0] + near[0, 0] + near[1, 0]).astype(BF16)
-    gi_ref[:, nk:] = (part[c, 1, 0] + mid[1] + near[0, 1] + near[1, 1]).astype(BF16)
+
+    def gi_piece(k):
+        for cp in rs:
+            if cp[0] == k:
+                cp[1].wait_recv()
+        cols = pl.ds(k * nk, nk)
+        gi_ref[:, cols] = (part[c, k, 1 - k] + mid[k] + near[0, k] + near[1, k]).astype(BF16)
+
+    for j in (2, 0):
+        gw_piece(j)
+    gi_piece(1)
+    gw_piece(3)
+    gi_piece(0)
+    gw_piece(1)
 
     for b in range(NH):
         for j in range(nj):
@@ -436,23 +446,19 @@
         ac(r, c).wait_send()
     for j in range(nj):
         ws(j).wait_send()
-    for cp in ax + rs:
+    for cp in ax + [cp for _, cp in rs]:
         cp.wait_send()
     pair_copy(0).wait_send()
     pair_copy(1).wait_send()
 
 
-def finish(gi_in, gw_in, gi_out, gw_out, gi_buf, gw_buf, sems):
-    pairs = ((gw_in, gw_buf, gw_out), (gi_in, gi_buf, gi_out))
-    into = [pltpu.make_async_copy(a, b, sems.at[k, 0]) for k, (a, b, _) in enumerate(pairs)]
-    outof = [pltpu.make_async_copy(b, o, sems.at[k, 1]) for k, (_, b, o) in enumerate(pairs)]
-    for cp in into:
-        cp.start()
-    for cp, out in zip(into, outof):
-        cp.wait()
-        out.start()
-    for out in outof:
-        out.wait()
+def finish(gi_in, gw_in, gi_out, gw_out, sems):
+    a = pltpu.make_async_copy(gi_in, gi_out, sems.at[0])
+    b = pltpu.make_async_copy(gw_in, gw_out, sems.at[1])
+    b.start()
+    a.start()
+    a.wait()
+    b.wait()
 
 
 def shards(acts, grad_out, weight):
@@ -468,8 +474,8 @@
     gi, gw = pl.pallas_call(
         kernel,
         out_shape=(
-            jax.ShapeDtypeStruct((frames, width), BF16),
-            jax.ShapeDtypeStruct((1, kb, hidden), BF16),
+            pltpu.VMEM((frames, width), BF16),
+            pltpu.VMEM((1, kb, hidden), BF16),
         ),
         in_specs=[pl.BlockSpec(memory_space=pl.ANY)] * 3,
         out_specs=(pl.BlockSpec(memory_space=pltpu.VMEM),) * 2,
@@ -491,18 +497,18 @@
         ]
         + [dma((n,)) for n in counts],
         compiler_params=pltpu.CompilerParams(
-            collective_id=0, has_side_effects=True, vmem_limit_bytes=62 << 20
+            collective_id=0, has_side_effects=True, vmem_limit_bytes=58 << 20
         ),
         name="grads",
     )(acts, grad_out, weight)
     return pl.pallas_call(
         finish,
         out_shape=(jax.ShapeDtypeStruct(gi.shape, BF16), jax.ShapeDtypeStruct(gw.shape, BF16)),
-        in_specs=[pl.BlockSpec(memory_space=pl.ANY)] * 2,
+        in_specs=[pl.BlockSpec(memory_space=pltpu.VMEM)] * 2,
         out_specs=(pl.BlockSpec(memory_space=pl.ANY),) * 2,
-        scratch_shapes=[pltpu.VMEM(gi.shape, BF16), pltpu.VMEM(gw.shape, BF16), dma((2, 2))],
+        scratch_shapes=[dma((2,))],
         name="finish",
-    )(gi, gw)
+    )(pltpu.with_memory_space_constraint(gi, pltpu.VMEM), pltpu.with_memory_space_constraint(gw, pltpu.VMEM))
 
 
 def solution(mesh):

time: 94.8 us -> 92.4 us (0.975)
  Pallas kernels: 93 us -> 90.8 us
    pallas_call x1, Pallas kernels: 2.22 us -> 1.03 us  [shards(): pl.pallas_call(finish, out_shape=(jax.ShapeDtypeStruct(gi.shape, BF16), j...]
    pallas_call x1, Pallas kernels: 90.8 us -> 89.8 us  [shards(): pl.pallas_call(kernel, out_shape=(pltpu.VMEM((frames, width), BF16), pltp...]
where the time goes in v5:
time: 92.4 us; the launch traced here: 91.4 us
  Pallas kernels  90.8 us (98%)
    pallas_call x1, Pallas kernels, shards(): pl.pallas_call(kernel, out_shape=(pltpu.VMEM((frames, width), BF16), pltp...  89.8 us

profile of v5, /device:TPU:1, one launch (start us, length us, event | category | flops | bytes accessed | tf_op | source)
XLA Modules:
  0.0 91.4 jit_solution(15960023314097412346)
XLA Ops:
  0.6 89.8 %grads.1 = (bf16[64,2048]{1,0:T(8,128)(2,1)S(1)}, bf16[1,256,1792]{2,1,0:T(8,128)(2,1)S(1)}) custom-call(bf16[64,2048]{1,0:T(8,128)(2,1)} %acts_hbm.1, bf16[128,1792]{1,0:T(8,128)(2,1)} %grad_hbm.1, bf16[2048,1792]{1,0:T(8,128)(2,1)} %w_hbm.1), custom_call_target="tpu_custom_call" | custom-call | tf_op jit(solution)/shard_map/grads/pallas_call | solution.py:474
  90.4 1.0 %finish.1 = (bf16[64,2048]{1,0:T(8,128)(2,1)}, bf16[1,256,1792]{2,1,0:T(8,128)(2,1)}) custom-call(bf16[64,2048]{1,0:T(8,128)(2,1)S(1)} %get-tuple-element.4.gi_in, bf16[1,256,1792]{2,1,0:T(8,128)(2,1)S(1)} %get-tuple-element.5.gw_in), custom_call_target="tpu_custom_call" | custom-call | tf_op jit(solution)/shard_map/finish/pallas_call | solution.py:504

commit v6 on v5

--- a/solution.py
+++ b/solution.py
@@ -13,7 +13,7 @@
 NX = NY = NL = 4
 NH = 2
 NZ = NH * NL
-TILE = 512
+TILE = 1024
 
 
 def chunks_of(hidden):
@@ -223,7 +223,7 @@
         )
 
     def acts_z(r):
-        for s in (1, NZ - 1, 2, NZ - 2, 3, NZ - 3, 4):
+        for s in (4, 3, NZ - 3, 2, NZ - 2, 1, NZ - 1):
             b = at_z(s) // NL
             remote(
                 xbuf.at[b, r], aall.at[r, c, (b + h) % 2, :, l], az_send, az_recv, r * NZ + s, dev_z(s)

time: 92.4 us -> 91.8 us (level)
  no operation moved by 1% of the time
where the time goes in v6:
time: 91.8 us; the launch traced here: 91.5 us
  Pallas kernels  90.8 us (99%)
    pallas_call x1, Pallas kernels, shards(): pl.pallas_call(kernel, out_shape=(pltpu.VMEM((frames, width), BF16), pltp...  89.8 us

profile of v6, /device:TPU:1, one launch (start us, length us, event | category | flops | bytes accessed | tf_op | source)
XLA Modules:
  0.0 91.5 jit_solution(14504504808650485221)
XLA Ops:
  0.6 89.8 %grads.1 = (bf16[64,2048]{1,0:T(8,128)(2,1)S(1)}, bf16[1,256,1792]{2,1,0:T(8,128)(2,1)S(1)}) custom-call(bf16[64,2048]{1,0:T(8,128)(2,1)} %acts_hbm.1, bf16[128,1792]{1,0:T(8,128)(2,1)} %grad_hbm.1, bf16[2048,1792]{1,0:T(8,128)(2,1)} %w_hbm.1), custom_call_target="tpu_custom_call" | custom-call | tf_op jit(solution)/shard_map/grads/pallas_call | solution.py:474
  90.4 1.0 %finish.1 = (bf16[64,2048]{1,0:T(8,128)(2,1)}, bf16[1,256,1792]{2,1,0:T(8,128)(2,1)}) custom-call(bf16[64,2048]{1,0:T(8,128)(2,1)S(1)} %get-tuple-element.4.gi_in, bf16[1,256,1792]{2,1,0:T(8,128)(2,1)S(1)} %get-tuple-element.5.gw_in), custom_call_target="tpu_custom_call" | custom-call | tf_op jit(solution)/shard_map/finish/pallas_call | solution.py:504

commit v7 on v6

--- a/solution.py
+++ b/solution.py
@@ -285,7 +285,7 @@
         return out
 
     def hx(j):
-        for cp in ch[0][j].hx:
+        for cp in ch[0][j].hx[::-1]:
             cp.start()
 
     rs = []

time: 91.8 us -> 91.6 us (level)
  no operation moved by 1% of the time
where the time goes in v7:
time: 91.6 us; the launch traced here: 91.5 us
  Pallas kernels  90.9 us (99%)
    pallas_call x1, Pallas kernels, shards(): pl.pallas_call(kernel, out_shape=(pltpu.VMEM((frames, width), BF16), pltp...  89.9 us

profile of v7, /device:TPU:1, one launch (start us, length us, event | category | flops | bytes accessed | tf_op | source)
XLA Modules:
  0.0 91.5 jit_solution(16365358607275990979)
XLA Ops:
  0.6 89.9 %grads.1 = (bf16[64,2048]{1,0:T(8,128)(2,1)S(1)}, bf16[1,256,1792]{2,1,0:T(8,128)(2,1)S(1)}) custom-call(bf16[64,2048]{1,0:T(8,128)(2,1)} %acts_hbm.1, bf16[128,1792]{1,0:T(8,128)(2,1)} %grad_hbm.1, bf16[2048,1792]{1,0:T(8,128)(2,1)} %w_hbm.1), custom_call_target="tpu_custom_call" | custom-call | tf_op jit(solution)/shard_map/grads/pallas_call | solution.py:474
  90.5 1.0 %finish.1 = (bf16[64,2048]{1,0:T(8,128)(2,1)}, bf16[1,256,1792]{2,1,0:T(8,128)(2,1)}) custom-call(bf16[64,2048]{1,0:T(8,128)(2,1)S(1)} %get-tuple-element.4.gi_in, bf16[1,256,1792]{2,1,0:T(8,128)(2,1)S(1)} %get-tuple-element.5.gw_in), custom_call_target="tpu_custom_call" | custom-call | tf_op jit(solution)/shard_map/finish/pallas_call | solution.py:504
